TPU v7x, 256 devices: a whole 4x4x8 slice. The times are simulated.
256 devices in a mesh: section: 16 (over z, x_hi), fsdp: 16 (over x_lo, y, core).
Axes of the slice: x: 4 (x_hi: 2, x_lo: 2; x = x_hi * 2 + x_lo), y: 4, z: 8, core: 2. Of those that a mesh axis runs over, the one named last changes fastest.
Arguments:
- x_fwd: bfloat16 [16, 384, 4096], P('section', None, 'fsdp'), may hold values from -6 to 6
- x_saved: bfloat16 [16, 384, 4096], P('section', None, 'fsdp'), may hold values from -6 to 6
- cotangent: bfloat16 [16, 384, 4096], P('section', None, 'fsdp'), may hold values from -6 to 6
- qkv_weight: bfloat16 [16, 4096, 3, 4096], P('section', None, None, 'fsdp')
- gain: float32 [16, 4096], P('section', 'fsdp'), may hold values from 0.1 to 1.9
- block_lists: int32 [8, 3, 2], replicated, may hold values from 0 to 2, as said below
- plan: int32 [16, 2], P('section'), may hold values from 0 to 7
Outputs:
- y_next: bfloat16 [16, 384, 4096], P('section', None, 'fsdp')
- dx_prev: bfloat16 [16, 384, 4096], P('section', None, 'fsdp')
- w_grad: bfloat16 [16, 4096, 3, 4096], P('section', None, None, 'fsdp')
- gain_grad: float32 [16, 4096], P('section', 'fsdp')
Inputs may be any that keep to these rules, and one draw needn't show every extreme that they name: block_lists[z, b, 0] = b; the 2 entries of a row are distinct.
All inputs are finite; a program needn't handle non-finite values.
Results may differ from a plain program's by a relative error of at most 0.024.
Values may be sent and summed in bfloat16 or wider, within the bound.
No kernel may reach another device: no remote copies, remote signals or barrier semaphores. Data moves between devices by JAX's collectives and lax.ppermute only.
A program may use at most 128 MiB of HBM per device.

v0:
```python
import math
import jax
import jax.numpy as jnp
from jax import lax
from jax.sharding import PartitionSpec as P

HD = 128
BLK = 128
EPS = 1e-05


def shifted(block, axis, distance):
    devices = range(lax.axis_size(axis))
    route = [((i - distance) % len(devices), i) for i in devices]
    return lax.ppermute(block, axis, route)


def attend(query, key_in, value, block_ids):
    tokens, feat_width = query.shape
    head_count = feat_width // HD
    block_count = tokens // BLK
    band_size = block_ids.shape[1]
    q_blocks = query.reshape(block_count, BLK, head_count, HD)
    k_rows = key_in.reshape(block_count, BLK, head_count, HD)[block_ids].reshape(
        block_count, band_size * BLK, head_count, HD
    )
    v_rows = value.reshape(block_count, BLK, head_count, HD)[block_ids].reshape(
        block_count, band_size * BLK, head_count, HD
    )
    scores = jnp.einsum("qthd,qshd->qhts", q_blocks, k_rows, preferred_element_type=jnp.float32) * (
        1.0 / math.sqrt(HD)
    )
    row_max = jnp.max(scores, axis=3, keepdims=True)
    expd = jnp.exp(scores - row_max)
    probs = expd / jnp.sum(expd, axis=3, keepdims=True)
    probs_low = probs.astype(jnp.bfloat16)
    output = jnp.einsum(
        "qhts,qshd->qthd", probs_low, v_rows, preferred_element_type=jnp.float32
    ).reshape(tokens, feat_width)
    return (output, (probs, probs_low, q_blocks, k_rows, v_rows))


def attend_back(upstream, block_ids, saved):
    probs, probs_low, q_blocks, k_rows, v_rows = saved
    block_count, block_len, head_count, head_size = q_blocks.shape
    band_size = block_ids.shape[1]
    tokens = block_count * block_len
    c_blocks = upstream.reshape(block_count, block_len, head_count, head_size)
    grad_vrows = jnp.einsum(
        "qhts,qthd->qshd", probs_low, c_blocks, preferred_element_type=jnp.float32
    )
    grad_p = jnp.einsum("qthd,qshd->qhts", c_blocks, v_rows, preferred_element_type=jnp.float32)
    grad_s = (
        probs * (grad_p - jnp.sum(probs * grad_p, axis=3, keepdims=True)) * (1.0 / math.sqrt(HD))
    )
    grad_s_low = grad_s.astype(jnp.bfloat16)
    grad_q = jnp.einsum("qhts,qshd->qthd", grad_s_low, k_rows, preferred_element_type=jnp.float32)
    grad_krows = jnp.einsum(
        "qhts,qthd->qshd", grad_s_low, q_blocks, preferred_element_type=jnp.float32
    )
    onehot = (
        block_ids[:, :, None] == jnp.arange(block_count, dtype=jnp.int32)[None, None, :]
    ).astype(jnp.float32)
    band_shape = (block_count, band_size, block_len, head_count, head_size)
    grad_k = jnp.einsum("qbk,qbthd->kthd", onehot, grad_krows.reshape(band_shape))
    grad_v = jnp.einsum("qbk,qbthd->kthd", onehot, grad_vrows.reshape(band_shape))
    return (grad_q.reshape(tokens, -1), grad_k.reshape(tokens, -1), grad_v.reshape(tokens, -1))


def on_device(x_fwd, x_saved, cotangent, qkv_weight, gain, block_lists, plan):
    forward_in = x_fwd[0]
    saved_in = x_saved[0]
    upstream = cotangent[0]
    weight = qkv_weight[0]
    gain_row = gain[0]
    full_width = weight.shape[0]
    local = weight.shape[2]
    tokens = forward_in.shape[0]
    w_flat = weight.reshape(full_width, 3 * local)
    lists_fwd = block_lists[plan[0, 0]]
    lists_bwd = block_lists[plan[0, 1]]
    wide_fwd = forward_in.astype(jnp.float32)
    wide_bwd = saved_in.astype(jnp.float32)
    scaled_fwd = (wide_fwd * gain_row[None, :]).astype(jnp.bfloat16)
    scaled_bwd = (wide_bwd * gain_row[None, :]).astype(jnp.bfloat16)
    sq_fwd, sq_bwd = lax.psum(
        (jnp.sum(wide_fwd * wide_fwd, axis=1), jnp.sum(wide_bwd * wide_bwd, axis=1)), "fsdp"
    )
    scale_fwd = lax.rsqrt(sq_fwd / full_width + EPS)
    scale_bwd = lax.rsqrt(sq_bwd / full_width + EPS)
    product_fwd = jnp.dot(
        lax.all_gather(scaled_fwd, "fsdp", axis=1, tiled=True),
        w_flat,
        preferred_element_type=jnp.float32,
    )
    whole_bwd = lax.all_gather(scaled_bwd, "fsdp", axis=1, tiled=True)
    product_bwd = jnp.dot(whole_bwd, w_flat, preferred_element_type=jnp.float32)
    proj_fwd = (scale_fwd[:, None] * product_fwd).astype(jnp.bfloat16)
    attn_fwd = attend(
        proj_fwd[:, :local], proj_fwd[:, local : 2 * local], proj_fwd[:, 2 * local :], lists_fwd
    )[0]
    result = (wide_fwd + attn_fwd).astype(jnp.bfloat16)
    sent_on = shifted(result[None], "section", 1)
    proj_bwd = (scale_bwd[:, None] * product_bwd).astype(jnp.bfloat16)
    saved = attend(
        proj_bwd[:, :local], proj_bwd[:, local : 2 * local], proj_bwd[:, 2 * local :], lists_bwd
    )[1]
    grad_q, grad_k, grad_v = attend_back(upstream, lists_bwd, saved)
    stacked = jnp.stack([grad_q, grad_k, grad_v], axis=1).reshape(tokens, 3 * local)
    grads = (scale_bwd[:, None] * stacked).astype(jnp.bfloat16)
    grad_w = lax.dot_general(
        whole_bwd, grads, (((0,), (0,)), ((), ())), preferred_element_type=jnp.float32
    )
    grad_w = grad_w.astype(jnp.bfloat16).reshape(1, full_width, 3, local)
    partial_in = lax.dot_general(
        grads, w_flat, (((1,), (1,)), ((), ())), preferred_element_type=jnp.float32
    )
    summed_in = lax.psum(partial_in.astype(jnp.bfloat16), "fsdp").astype(jnp.float32)
    own_in = lax.dynamic_slice_in_dim(summed_in, lax.axis_index("fsdp") * local, local, 1)
    row_total = jnp.sum(whole_bwd.astype(jnp.float32) * summed_in, axis=1)
    grad_x = upstream.astype(jnp.float32) + gain_row[None, :] * own_in
    grad_x = grad_x - (scale_bwd * scale_bwd * row_total / full_width)[:, None] * wide_bwd
    sent_back = shifted(grad_x.astype(jnp.bfloat16)[None], "section", -1)
    grad_gain = jnp.sum(wide_bwd * own_in, axis=0)[None]
    return (sent_on, sent_back, grad_w, grad_gain)


def solution(mesh):
    in_specs = (
        P("section", None, "fsdp"),
        P("section", None, "fsdp"),
        P("section", None, "fsdp"),
        P("section", None, None, "fsdp"),
        P("section", "fsdp"),
        P(),
        P("section", None),
    )
    out_specs = (
        P("section", None, "fsdp"),
        P("section", None, "fsdp"),
        P("section", None, None, "fsdp"),
        P("section", "fsdp"),
    )
    return jax.shard_map(
        on_device, mesh=mesh, in_specs=in_specs, out_specs=out_specs, check_vma=False
    )
```

profile of v0, /device:TPU:25, one launch (start us, length us, event | category | flops | bytes accessed | tf_op | source)
XLA Modules:
  0.0 275.0 jit_solution(14417627607529717031)
XLA Ops:
  7.2 1.9 fusion.21
  9.1 0.7 all-gather.3.cloned.1.call-update
  9.9 1.3 fusion.70
  13.7 8.7 %copy.55 = bf16[1,4096,3,256]{1,3,2,0:T(8,128)(2,1)} copy(bf16[1,4096,3,256]{3,1,2,0:T(8,128)(2,1)} %param.10) | data formatting | bytes 12582912 | tf_op args[3]
  24.1 26.6 %all-reduce = (f32[384]{0:T(512)S(1)}, f32[384]{0:T(512)S(1)}) all-reduce(f32[384]{0:T(512)S(1)} %get-tuple-element.28, f32[384]{0:T(512)S(1)} %get-tuple-element.32), channel_id=1, replica_groups=mesh['section'=16,'fsdp'=16] {'fsdp'}, use_global_device_ids=true, to_apply=%region_1.0 | all-reduce | flops 768 | bytes 6144 | tf_op jit(solution)/shard_map/psum | solution.py:86
  50.7 5.6 %all-gather.5.cloned.1.call-done = bf16[384,4096]{1,0:T(8,128)(2,1)} async-done(((bf16[384,256]{1,0:T(8,128)(2,1)}), bf16[384,4096]{1,0:T(8,128)(2,1)}) %all-gather.5.cloned.1.call-update) | async-done | bytes 3145744 | tf_op jit(solution)/shard_map/all_gather | solution.py:96
  56.3 6.4 %fusion.6 = bf16[384,768]{1,0:T(8,128)(2,1)S(1)} fusion(bf16[384,4096]{1,0:T(8,128)(2,1)} %all-gather.5.cloned.1.call-done, bf16[4096,768]{0,1:T(8,128)(2,1)} %bitcast.81, f32[384]{0:T(512)S(1)} %add_rsqrt_fusion), kind=kOutput, calls=%fused_computation.15 | convolution fusion | flops 2416508928 | bytes 10028544 | tf_op jit(solution)/shard_map/dot_general | solution.py:97
  62.8 0.6 gather_fusion.3
  63.6 0.6 gather_fusion.2
  64.3 0.2 copy.80
  64.5 0.3 convolution_bitcast_fusion.1
  64.8 1.3 fusion.76
  66.1 5.9 %convolution_bitcast_fusion.4 = f32[3,128,2,128]{1,3,2,0:T(8,128)S(1)} fusion(f32[3,2,128,256]{3,2,1,0:T(8,128)S(1)} %convolution_bitcast_fusion.1, bf16[3,256,2,128]{3,1,0,2:T(8,128)(2,1)S(1)} %bitcast.91, f32[3,2,128,256]{3,2,1,0:T(8,128)} %get-tuple-element.37, f32[3,2,128]{2,1,0:T(2,128)S(1)} %get-tuple-element.36), kind=kOutput, calls=%fused_computation.28 | convolution fusion | flops 51708928 | bytes 2362368 | tf_op jit(solution)/shard_map/qhts,qshd->qthd/dot_general | solution.py:57
  72.0 0.2 copy.78
  72.2 0.3 stack_reshape.9
  72.5 5.4 %convolution_bitcast_fusion = bf16[3,256,2,128]{1,3,2,0:T(8,128)(2,1)S(1)} fusion(bf16[3,128,2,128]{1,3,2,0:T(8,128)(2,1)S(1)} %copy.80, f32[3,2,128,256]{3,2,1,0:T(8,128)S(1)} %convolution_bitcast_fusion.1, f32[3,2,128,256]{3,2,1,0:T(8,128)} %get-tuple-element.37, f32[3,2,128]{2,1,0:T(2,128)S(1)} %get-tuple-element.36), kind=kOutput, calls=%fused_computation.21 | convolution fusion | flops 51708928 | bytes 2165760 | tf_op jit(solution)/shard_map/qhts,qthd->qshd/dot_general | solution.py:58
  78.0 0.7 copy.81
  78.7 0.5 convolution_bitcast_fusion.3
  79.2 0.2 copy.82
  79.4 0.3 stack_reshape.10
  79.8 1.7 fusion.32
  81.5 0.6 convolution_bitcast_fusion.2
  82.1 0.2 copy.86
  82.3 0.3 stack_reshape.11
  82.9 0.3 copy.87
  83.2 7.1 %convolution_convert_fusion.1 = bf16[384,4096]{1,0:T(8,128)(2,1)} fusion(bf16[384,768]{0,1:T(8,128)(2,1)S(1)} %bitcast.86, bf16[4096,768]{0,1:T(8,128)(2,1)} %bitcast.82), kind=kOutput, calls=%fused_computation.9 | convolution fusion | flops 2417491968 | bytes 10027008 | tf_op jit(solution)/shard_map/dot_general | solution.py:115
  90.6 0.4 copy.88
  90.9 11.8 %all-gather.3.cloned.1.call-done = bf16[384,4096]{1,0:T(8,128)(2,1)} async-done(((bf16[384,256]{1,0:T(8,128)(2,1)}), bf16[384,4096]{1,0:T(8,128)(2,1)}) %all-gather.3.cloned.1.call-update) | async-done | bytes 3145744 | tf_op jit(solution)/shard_map/all_gather | solution.py:92
  102.7 6.4 %fusion.5 = bf16[384,768]{1,0:T(8,128)(2,1)S(1)} fusion(bf16[384,4096]{1,0:T(8,128)(2,1)} %all-gather.3.cloned.1.call-done, bf16[4096,768]{0,1:T(8,128)(2,1)} %bitcast.83, f32[384]{0:T(512)S(1)} %add_rsqrt_fusion.1), kind=kOutput, calls=%fused_computation.14 | convolution fusion | flops 2416508928 | bytes 10028544 | tf_op jit(solution)/shard_map/dot_general | solution.py:91
  109.2 0.6 gather_fusion
  109.9 0.8 copy.59
  110.7 0.6 gather_fusion.1
  111.5 0.5 fusion.71
  112.0 0.3 convolution_multiply_fusion.3
  112.4 1.6 convolution_bitcast_fusion.5
  114.0 0.2 copy.65
  114.2 0.3 reshape.154
  114.6 3.2 %collective-permute-start = (bf16[1,384,256]{2,1,0:T(8,128)(2,1)S(1)}, bf16[1,384,256]{2,1,0:T(8,128)(2,1)S(1)}, u32[]{:S(2)}, u32[]{:S(2)}) collective-permute-start(bf16[1,384,256]{2,1,0:T(8,128)(2,1)S(1)} %fusion.23), channel_id=1, source_target_pairs={{240,0},{0,16},{16,32},{32,48},{48,64},{64,80},{80,96},{96,112},{1... | collective-permute-start | bytes 589832 | tf_op jit(solution)/shard_map/ppermute | solution.py:15
  117.8 0.4 copy.89
  118.2 123.7 %all-reduce.3.cloned.1.call-done = bf16[384,4096]{1,0:T(8,128)(2,1)} async-done(((bf16[384,4096]{1,0:T(8,128)(2,1)}), bf16[384,4096]{1,0:T(8,128)(2,1)}) %all-reduce.3.cloned.1.call-update) | async-done | bytes 3145744 | tf_op jit(solution)/shard_map/psum | solution.py:118
  241.9 3.9 %multiply_reduce_fusion = f32[384]{0:T(512)S(1)} fusion(bf16[384,4096]{1,0:T(8,128)(2,1)} %all-gather.5.cloned.1.call-done, bf16[384,4096]{1,0:T(8,128)(2,1)} %all-reduce.3.cloned.1.call-done), kind=kLoop, calls=%fused_computation.8 | loop fusion | flops 6291072 | bytes 6292992 | tf_op jit(solution)/shard_map/reduce_sum | solution.py:120
  245.8 0.8 convert_element_type.94
  246.7 0.7 fusion.28
  247.4 5.4 %collective-permute-start.1 = (bf16[1,384,256]{2,1,0:T(8,128)(2,1)S(1)}, bf16[1,384,256]{2,1,0:T(8,128)(2,1)S(1)}, u32[]{:S(2)}, u32[]{:S(2)}) collective-permute-start(bf16[1,384,256]{2,1,0:T(8,128)(2,1)S(1)} %get-tuple-element.19), channel_id=1, source_target_pairs={{16,0},{32,16},{48,32},{64,48},{80,64},{96,80},{112,96},{128,112},... | collective-permute-start | bytes 589832 | tf_op jit(solution)/shard_map/ppermute | solution.py:15
  252.9 5.6 %convolution_convert_fusion = bf16[4096,768]{0,1:T(8,128)(2,1)} fusion(bf16[384,4096]{1,0:T(8,128)(2,1)S(1)} %copy-done.1, f32[384,768]{1,0:T(8,128)S(1)} %copy.89, f32[384]{0:T(512)S(1)} %add_rsqrt_fusion), kind=kOutput, calls=%fused_computation.7 | convolution fusion | flops 2419654656 | bytes 10618368 | tf_op jit(solution)/shard_map/dot_general | solution.py:111
  258.5 8.6 %copy.90 = bf16[1,4096,3,256]{3,1,2,0:T(8,128)(2,1)} copy(bf16[1,4096,3,256]{1,3,2,0:T(8,128)(2,1)} %bitcast.84) | data formatting | bytes 12582912
  267.1 0.7 copy.141
  267.8 0.7 copy.142
  (58 shorter events, 2.1 us)
Async XLA Ops:
  7.2 49.1 %all-gather.5.cloned.1.call-start = ((), (), s32[]{:S(2)}) async-start(), calls=%async_computation.1 | async-start | bytes 3342336 | tf_op jit(solution)/shard_map/all_gather | solution.py:96
  9.1 93.6 %all-gather.3.cloned.1.call-start = ((), (), s32[]{:S(2)}) async-start(), calls=%async_computation | async-start | bytes 3342336 | tf_op jit(solution)/shard_map/all_gather | solution.py:92
  9.8 232.1 %all-reduce.3.cloned.1.call-start = ((), (), s32[]{:S(2)}) async-start(), calls=%async_computation.2 | async-start | bytes 6291456 | tf_op jit(solution)/shard_map/psum | solution.py:118
  13.6 9.9 %copy-start.6 = (s32[8,3,2]{0,2,1:T(2,128)S(1)}, s32[8,3,2]{0,2,1:T(2,128)}, u32[]{:S(2)}) copy-start(s32[8,3,2]{0,2,1:T(2,128)} %param.12) | copy-start | bytes 580
  13.7 10.4 %copy-start.2 = (bf16[1,384,256]{2,1,0:T(8,128)(2,1)S(1)}, bf16[1,384,256]{2,1,0:T(8,128)(2,1)}, u32[]{:S(2)}) copy-start(bf16[1,384,256]{2,1,0:T(8,128)(2,1)} %param.9) | copy-start | bytes 589828
  111.4 1.0 copy-start.5
  111.9 2.6 copy-start.4
  114.6 152.4 %collective-permute-start = (bf16[1,384,256]{2,1,0:T(8,128)(2,1)S(1)}, bf16[1,384,256]{2,1,0:T(8,128)(2,1)S(1)}, u32[]{:S(2)}, u32[]{:S(2)}) collective-permute-start(bf16[1,384,256]{2,1,0:T(8,128)(2,1)S(1)} %fusion.23), channel_id=1, source_target_pairs={{240,0},{0,16},{16,32},{32,48},{48,64},{64,80},{80,96},{96,112},{1... | collective-permute-start | bytes 589832 | tf_op jit(solution)/shard_map/ppermute | solution.py:15
  241.9 3.9 %copy-start = (bf16[384,4096]{1,0:T(8,128)(2,1)S(1)}, bf16[384,4096]{1,0:T(8,128)(2,1)}, u32[]{:S(2)}) copy-start(bf16[384,4096]{1,0:T(8,128)(2,1)} %all-reduce.3.cloned.1.call-done) | copy-start | bytes 9437188
  245.8 0.9 copy-start.3
  245.8 0.9 copy-start.7
  245.8 7.1 %copy-start.1 = (bf16[384,4096]{1,0:T(8,128)(2,1)S(1)}, bf16[384,4096]{1,0:T(8,128)(2,1)}, u32[]{:S(2)}) copy-start(bf16[384,4096]{1,0:T(8,128)(2,1)} %all-gather.5.cloned.1.call-done) | copy-start | bytes 9437188
  247.4 19.6 %collective-permute-start.1 = (bf16[1,384,256]{2,1,0:T(8,128)(2,1)S(1)}, bf16[1,384,256]{2,1,0:T(8,128)(2,1)S(1)}, u32[]{:S(2)}, u32[]{:S(2)}) collective-permute-start(bf16[1,384,256]{2,1,0:T(8,128)(2,1)S(1)} %get-tuple-element.19), channel_id=1, source_target_pairs={{16,0},{32,16},{48,32},{64,48},{80,64},{96,80},{112,96},{128,112},... | collective-permute-start | bytes 589832 | tf_op jit(solution)/shard_map/ppermute | solution.py:15
Sparse Core Ops, SparseCore 0:
  10.3 45.9 all-gather.4
  58.7 44.0 all-gather.2
  105.4 136.4 all-reduce.2
where the time goes:
time: 276 us; the launch traced here: 275 us
  waiting for transfers between devices  142 us (51%)
  matrix products  43.6 us (16%)
  local copies, waits for them, and re-layouts  29 us (11%)
  blocking collectives  26.6 us (10%)
  between operations  17.8 us (6%)
  starting transfers between devices  8.75 us (3%)
  other arithmetic  7.41 us (3%)
    psum x1, waiting for transfers between devices, on_device(): lax.psum(partial_in.astype(jnp.bfloat16), 'fsdp').astype(jnp.float32)  124 us
    psum x1, blocking collectives, on_device(): lax.psum((jnp.sum(wide_fwd * wide_fwd, axis=1), jnp.sum(wide_bwd * wide_b...  26.6 us
    unnamed x22, local copies, waits for them, and re-layouts  19 us
    all_gather x1, waiting for transfers between devices, on_device(): lax.all_gather(scaled_fwd, 'fsdp', axis=1, tiled=True)  11.8 us
    ppermute x2, starting transfers between devices, shifted(): return lax.ppermute(block, axis, route)  8.63 us
    dot_general x1, matrix products, on_device(): lax.dot_general(grads, w_flat, (((1,), (1,)), ((), ())), preferred_elemen...  7.14 us
    dot_general x1, matrix products, on_device(): jnp.dot(lax.all_gather(scaled_fwd, 'fsdp', axis=1, tiled=True), w_flat, p...  6.37 us
    dot_general x1, matrix products, on_device(): product_bwd = jnp.dot(whole_bwd, w_flat, preferred_element_type=jnp.float32)  6.37 us
  transfers between devices with their start and end apart: 5, of which 3 were waited for; matrix products, arithmetic and copies ran while one was open for 28% of the time, Pallas kernels for 0%

commit v1 on v0

--- a/solution.py
+++ b/solution.py
@@ -93,7 +93,9 @@
         w_flat,
         preferred_element_type=jnp.float32,
     )
-    whole_bwd = lax.all_gather(scaled_bwd, "fsdp", axis=1, tiled=True)
+    whole_bwd = jnp.concatenate(
+        lax.all_to_all(jnp.stack([scaled_bwd] * lax.axis_size("fsdp")), "fsdp", 0, 0), axis=1
+    )
     product_bwd = jnp.dot(whole_bwd, w_flat, preferred_element_type=jnp.float32)
     proj_fwd = (scale_fwd[:, None] * product_fwd).astype(jnp.bfloat16)
     attn_fwd = attend(

time: 276 us -> 330 us (1.20)
  local copies, waits for them, and re-layouts: 29 us -> 76.5 us
  waiting for transfers between devices: 142 us -> 103 us
  blocking collectives: 26.6 us -> 49.7 us
  matrix products: 43.6 us -> 55.3 us
  starting transfers between devices: 8.75 us -> 13.9 us
  other arithmetic: 7.41 us -> 11.9 us
    psum x1, blocking collectives: 26.6 us -> 49.7 us  [on_device(): lax.psum((jnp.sum(wide_fwd * wide_fwd, axis=1), jnp.sum(wide_bwd * wide_b...]
    psum x1, waiting for transfers between devices: 124 us -> 103 us  [on_device(): lax.psum(partial_in.astype(jnp.bfloat16), 'fsdp').astype(jnp.float32)]
    all_gather x1, waiting for transfers between devices: 11.8 us -> 0.02 us  [on_device(): lax.all_gather(scaled_fwd, 'fsdp', axis=1, tiled=True)]
    all_to_all x0 -> x1, starting transfers between devices: none -> 6.09 us  [on_device(): lax.all_to_all(jnp.stack([scaled_bwd] * lax.axis_size('fsdp')), 'fsdp', 0...]
    all_gather x1 -> x0, waiting for transfers between devices: 5.57 us -> none  [on_device(): whole_bwd = lax.all_gather(scaled_bwd, 'fsdp', axis=1, tiled=True)]
    unnamed x22 -> x46, local copies, waits for them, and re-layouts: 19 us -> 24.1 us
    gather x4, local copies, waits for them, and re-layouts: 1.3 us -> 6.23 us  [attend(): key_in.reshape(block_count, BLK, head_count, HD)[block_ids]]
    another operation x5 -> x3, local copies, waits for them, and re-layouts: 1.35 us -> 6.16 us  [on_device(): jnp.stack([grad_q, grad_k, grad_v], axis=1).reshape(tokens, 3 * local)]
  transfers between devices with their start and end apart: 5 -> 5, of which waited for: 3 -> 1; matrix products, arithmetic and copies ran while one was open for 28% -> 41% of each run, Pallas kernels for 0% -> 0%
where the time goes in v1:
time: 330 us; the launch traced here: 328 us
  waiting for transfers between devices  103 us (31%)
  local copies, waits for them, and re-layouts  76.5 us (23%)
  matrix products  55.3 us (17%)
  blocking collectives  49.7 us (15%)
  between operations  18.2 us (6%)
  starting transfers between devices  13.9 us (4%)
  other arithmetic  11.9 us (4%)
    psum x1, waiting for transfers between devices, on_device(): lax.psum(partial_in.astype(jnp.bfloat16), 'fsdp').astype(jnp.float32)  103 us
    psum x1, blocking collectives, on_device(): lax.psum((jnp.sum(wide_fwd * wide_fwd, axis=1), jnp.sum(wide_bwd * wide_b...  49.7 us
    unnamed x46, local copies, waits for them, and re-layouts  24.1 us
    ppermute x2, starting transfers between devices, shifted(): return lax.ppermute(block, axis, route)  7.75 us
    dot_general x1, matrix products, on_device(): lax.dot_general(grads, w_flat, (((1,), (1,)), ((), ())), preferred_elemen...  7.36 us
    dot_general x1, matrix products, attend_back(): jnp.einsum('qhts,qshd->qthd', grad_s_low, k_rows, preferred_element_type=...  7.36 us
    dot_general x1, matrix products, attend_back(): jnp.einsum('qhts,qthd->qshd', grad_s_low, q_blocks, preferred_element_typ...  6.69 us
  transfers between devices with their start and end apart: 5, of which 1 were waited for; matrix products, arithmetic and copies ran while one was open for 41% of the time, Pallas kernels for 0%

profile of v1, /device:TPU:25, one launch (start us, length us, event | category | flops | bytes accessed | tf_op | source)
XLA Modules:
  0.0 328.4 jit_solution(10628518043614622028)
XLA Ops:
  8.1 2.0 stack.7
  10.1 6.1 %all-to-all-start = ((bf16[16,384,256]{2,1,0:T(8,128)(2,1)}), bf16[16,384,256]{2,1,0:T(8,128)(2,1)S(1)}, u32[]{:S(2)}, u32[]{:S(2)}) async-start(bf16[16,384,256]{2,1,0:T(8,128)(2,1)} %stack.7), calls=%async_computation | async-start | bytes 6291456 | tf_op jit(solution)/shard_map/all_to_all | solution.py:97
  16.3 1.3 fusion.24
  20.9 8.7 %copy.87 = bf16[1,4096,3,256]{1,3,2,0:T(8,128)(2,1)} copy(bf16[1,4096,3,256]{3,1,2,0:T(8,128)(2,1)} %param.10) | data formatting | bytes 12582912 | tf_op args[3]
  33.9 49.7 %all-reduce = (f32[384]{0:T(512)}, f32[384]{0:T(512)S(1)}) all-reduce(f32[384]{0:T(512)} %get-tuple-element.30, f32[384]{0:T(512)} %get-tuple-element.38), channel_id=1, replica_groups=mesh['section'=16,'fsdp'=16] {'fsdp'}, use_global_device_ids=true, to_apply=%region_1.0 | all-reduce | flops 768 | bytes 6144 | tf_op jit(solution)/shard_map/psum | solution.py:86
  83.6 1.7 copy-done.1
  85.3 2.4 copy.131
  89.0 2.7 fusion.6
  92.5 1.7 reshape.190
  94.2 1.8 copy.113
  97.6 1.4 gather_fusion.2
  99.0 1.8 copy.102
  100.7 3.0 fusion.80
  103.7 3.7 %fusion.35 = bf16[3,2,256,128]{3,2,1,0:T(8,128)(2,1)} fusion(bf16[3,128,2,128]{3,2,1,0:T(2,128)(2,1)} %reshape_squeeze.7, f32[3,2,128]{2,1,0:T(2,128)} %get-tuple-element.36, bf16[3,128,2,128]{1,3,2,0:T(8,128)(2,1)} %copy.113, bf16[3,256,2,128]{3,1,0,2:T(8,128)(2,1)} %bitcast.112), kind=kOutput, calls=%fused_computation.58 | convolution fusion | flops 101450752 | bytes 1182720 | tf_op jit(solution)/shard_map/qhts,qthd->qshd/dot_general | solution.py:49
  107.4 1.6 convolution_bitcast_fusion.2
  110.0 2.1 stack_reshape.11
  113.7 1.4 gather_fusion.3
  116.1 2.1 convolution_bitcast_fusion.1
  118.2 6.7 %convolution_bitcast_fusion = bf16[3,256,2,128]{1,3,2,0:T(8,128)(2,1)} fusion(bf16[3,128,2,128]{1,3,2,0:T(8,128)(2,1)} %copy.113, f32[3,2,128,256]{3,2,1,0:T(8,128)} %convolution_bitcast_fusion.1, f32[3,2,128,256]{3,2,1,0:T(8,128)} %get-tuple-element.37, f32[3,2,128]{2,1,0:T(2,128)} %get-tuple-element.36), kind=kOutput, calls=%fused_computation.21 | convolution fusion | flops 51708928 | bytes 2165760 | tf_op jit(solution)/shard_map/qhts,qthd->qshd/dot_general | solution.py:58
  124.9 1.9 reshape.193
  126.8 2.1 copy.114
  128.9 1.5 convolution_bitcast_fusion.3
  131.4 2.1 stack_reshape.10
  133.5 7.4 %convolution_bitcast_fusion.4 = f32[3,128,2,128]{1,3,2,0:T(8,128)} fusion(f32[3,2,128,256]{3,2,1,0:T(8,128)} %convolution_bitcast_fusion.1, bf16[3,256,2,128]{3,1,0,2:T(8,128)(2,1)} %bitcast.113, f32[3,2,128,256]{3,2,1,0:T(8,128)} %get-tuple-element.37, f32[3,2,128]{2,1,0:T(2,128)S(1)} %copy-done.20), kind=kOutput, calls=%fused_computation.28 | convolution fusion | flops 51708928 | bytes 2362368 | tf_op jit(solution)/shard_map/qhts,qshd->qthd/dot_general | solution.py:57
  140.8 1.9 copy.111
  142.8 2.0 stack_reshape.9
  144.8 2.2 fusion.13
  147.0 2.1 copy.120
  149.1 7.4 %convolution_convert_fusion.1 = bf16[384,4096]{1,0:T(8,128)(2,1)} fusion(bf16[384,768]{0,1:T(8,128)(2,1)} %bitcast.106, bf16[4096,768]{0,1:T(8,128)(2,1)} %bitcast.98), kind=kOutput, calls=%fused_computation.9 | convolution fusion | flops 2417491968 | bytes 10027008 | tf_op jit(solution)/shard_map/dot_general | solution.py:117
  157.4 6.4 %fusion.5 = bf16[384,768]{1,0:T(8,128)(2,1)S(1)} fusion(bf16[384,4096]{1,0:T(8,128)(2,1)} %all-gather.2.cloned.1.call-done, bf16[4096,768]{0,1:T(8,128)(2,1)} %bitcast.99, f32[384]{0:T(512)S(1)} %add_rsqrt_fusion.1), kind=kOutput, calls=%fused_computation.14 | convolution fusion | flops 2416508928 | bytes 10028544 | tf_op jit(solution)/shard_map/dot_general | solution.py:91
  166.2 1.4 gather_fusion
  167.6 1.8 copy.91
  169.3 1.7 reshape.183
  172.0 1.4 gather_fusion.1
  173.3 1.8 copy.93
  176.8 1.5 fusion.75
  178.3 2.3 convolution_multiply_fusion.3
  180.6 3.9 %convolution_bitcast_fusion.5 = f32[3,128,2,128]{1,3,2,0:T(8,128)} fusion(bf16[3,256,2,128]{3,1,0,2:T(8,128)(2,1)} %bitcast.114, f32[3,2,128]{2,1,0:T(2,128)S(1)} %fusion.75, f32[3,2,128,256]{3,2,1,0:T(8,128)} %convolution_multiply_fusion.3), kind=kOutput, calls=%fused_computation.29 | convolution fusion | flops 50922496 | bytes 1575936 | tf_op jit(solution)/shard_map/qhts,qshd->qthd/dot_general | solution.py:37
  184.5 1.9 copy.97
  186.4 2.1 reshape.185
  188.4 1.7 fusion.26
  190.2 2.3 collective-permute-start
  192.5 102.8 %all-reduce.3.cloned.1.call-done = bf16[384,4096]{1,0:T(8,128)(2,1)} async-done(((bf16[384,4096]{1,0:T(8,128)(2,1)}), bf16[384,4096]{1,0:T(8,128)(2,1)}) %all-reduce.3.cloned.1.call-update) | async-done | bytes 3145744 | tf_op jit(solution)/shard_map/psum | solution.py:120
  295.3 2.9 multiply_reduce_fusion
  299.9 5.4 %collective-permute-start.1 = (bf16[1,384,256]{2,1,0:T(8,128)(2,1)S(1)}, bf16[1,384,256]{2,1,0:T(8,128)(2,1)S(1)}, u32[]{:S(2)}, u32[]{:S(2)}) collective-permute-start(bf16[1,384,256]{2,1,0:T(8,128)(2,1)S(1)} %get-tuple-element.23), channel_id=1, source_target_pairs={{16,0},{32,16},{48,32},{64,48},{80,64},{96,80},{112,96},{128,112},... | collective-permute-start | bytes 589832 | tf_op jit(solution)/shard_map/ppermute | solution.py:15
  305.3 5.3 %convolution_convert_fusion = bf16[4096,768]{0,1:T(8,128)(2,1)} fusion(bf16[384,768]{0,1:T(8,128)(2,1)S(1)} %bitcast.107, bf16[384,4096]{1,0:T(8,128)(2,1)S(1)} %bitcast.103), kind=kOutput, calls=%fused_computation.7 | convolution fusion | flops 2419064832 | bytes 10027008 | tf_op jit(solution)/shard_map/dot_general | solution.py:113
  310.6 8.6 %copy.121 = bf16[1,4096,3,256]{3,1,2,0:T(8,128)(2,1)} copy(bf16[1,4096,3,256]{1,3,2,0:T(8,128)(2,1)} %bitcast.105) | data formatting | bytes 12582912
  319.2 1.6 copy.171
  (81 shorter events, 21.4 us)
Async XLA Ops:
  10.1 6.2 %copy-start.4 = (bf16[1,384,256]{2,1,0:T(8,128)(2,1)S(1)}, bf16[1,384,256]{2,1,0:T(8,128)(2,1)}, u32[]{:S(2)}) copy-start(bf16[1,384,256]{2,1,0:T(8,128)(2,1)} %param.8) | copy-start | bytes 589828
  10.1 6.2 %copy-start.8 = (bf16[1,384,256]{2,1,0:T(8,128)(2,1)S(1)}, bf16[1,384,256]{2,1,0:T(8,128)(2,1)}, u32[]{:S(2)}) copy-start(bf16[1,384,256]{2,1,0:T(8,128)(2,1)} %param.7) | copy-start | bytes 589828
  10.1 6.2 %copy-start.12 = (f32[1,256]{1,0:T(1,128)S(1)}, f32[1,256]{1,0:T(1,128)}, u32[]{:S(2)}) copy-start(f32[1,256]{1,0:T(1,128)} %param.11) | copy-start | bytes 3076
  10.1 7.6 %copy-start.19 = (s32[1,2]{1,0:T(1,128)S(1)}, s32[1,2]{1,0:T(1,128)}, u32[]{:S(2)}) copy-start(s32[1,2]{1,0:T(1,128)} %param.13) | copy-start | bytes 28
  10.1 73.5 %all-to-all-start = ((bf16[16,384,256]{2,1,0:T(8,128)(2,1)}), bf16[16,384,256]{2,1,0:T(8,128)(2,1)S(1)}, u32[]{:S(2)}, u32[]{:S(2)}) async-start(bf16[16,384,256]{2,1,0:T(8,128)(2,1)} %stack.7), calls=%async_computation | async-start | bytes 6291456 | tf_op jit(solution)/shard_map/all_to_all | solution.py:97
  16.2 141.1 %all-gather.2.cloned.1.call-start = ((), (), s32[]{:S(2)}) async-start(), calls=%async_computation.1 | async-start | bytes 3342336 | tf_op jit(solution)/shard_map/all_gather | solution.py:92
  17.7 277.6 %all-reduce.3.cloned.1.call-start = ((), (), s32[]{:S(2)}) async-start(), calls=%async_computation.2 | async-start | bytes 6291456 | tf_op jit(solution)/shard_map/psum | solution.py:120
  20.9 10.0 %copy-start.11 = (s32[8,3,2]{0,2,1:T(2,128)S(1)}, s32[8,3,2]{0,2,1:T(2,128)}, u32[]{:S(2)}) copy-start(s32[8,3,2]{0,2,1:T(2,128)} %param.12) | copy-start | bytes 580
  20.9 10.8 %copy-start.5 = (bf16[1,384,256]{2,1,0:T(8,128)(2,1)S(1)}, bf16[1,384,256]{2,1,0:T(8,128)(2,1)}, u32[]{:S(2)}) copy-start(bf16[1,384,256]{2,1,0:T(8,128)(2,1)} %param.9) | copy-start | bytes 589828
  31.1 2.8 copy-start.13
  83.6 8.1 %copy-start.15 = (f32[384]{0:T(512)}, f32[384]{0:T(512)S(1)}, u32[]{:S(2)}) copy-start(f32[384]{0:T(512)S(1)} %add_rsqrt_fusion) | copy-start | bytes 4612
  83.6 1.7 copy-start.1
  85.3 3.7 %copy-start = (bf16[1,4096,3,256]{1,3,2,0:T(8,128)(2,1)S(1)}, bf16[1,4096,3,256]{1,3,2,0:T(8,128)(2,1)}, u32[]{:S(2)}) copy-start(bf16[1,4096,3,256]{1,3,2,0:T(8,128)(2,1)} %copy.87) | copy-start | bytes 18874372
  99.0 8.4 %copy-start.14 = (s32[1,3,2]{1,2,0:T(2,128)S(1)}, s32[1,3,2]{1,2,0:T(2,128)}, u32[]{:S(2)}) copy-start(s32[1,3,2]{1,2,0:T(2,128)} %copy-done.13) | copy-start | bytes 76
  103.7 8.3 %copy-start.7 = (bf16[384,256]{1,0:T(8,128)(2,1)S(1)}, bf16[384,256]{1,0:T(8,128)(2,1)}, u32[]{:S(2)}) copy-start(bf16[384,256]{1,0:T(8,128)(2,1)} %get-tuple-element.24) | copy-start | bytes 589828
  124.9 8.6 %copy-start.20 = (f32[3,2,128]{2,1,0:T(2,128)S(1)}, f32[3,2,128]{2,1,0:T(2,128)}, u32[]{:S(2)}) copy-start(f32[3,2,128]{2,1,0:T(2,128)} %get-tuple-element.36) | copy-start | bytes 9220
  131.4 13.4 %copy-start.16 = (f32[384]{0:T(512)S(1)}, f32[384]{0:T(512)}, u32[]{:S(2)}) copy-start(f32[384]{0:T(512)} %copy-done.15) | copy-start | bytes 4612
  156.4 0.7 copy-start.17
  156.4 0.9 copy-start.18
  176.1 0.7 copy-start.10
  178.3 10.2 %copy-start.9 = (bf16[1,384,256]{2,1,0:T(8,128)(2,1)S(1)}, bf16[1,384,256]{2,1,0:T(8,128)(2,1)}, u32[]{:S(2)}) copy-start(bf16[1,384,256]{2,1,0:T(8,128)(2,1)} %param.7) | copy-start | bytes 589828
  190.2 129.1 %collective-permute-start = (bf16[1,384,256]{2,1,0:T(8,128)(2,1)}, bf16[1,384,256]{2,1,0:T(8,128)(2,1)}, u32[]{:S(2)}, u32[]{:S(2)}) collective-permute-start(bf16[1,384,256]{2,1,0:T(8,128)(2,1)} %fusion.26), channel_id=1, source_target_pairs={{240,0},{0,16},{16,32},{32,48},{48,64},{64,80},{80,96},{96,112},{1... | collective-permute-start | bytes 589832 | tf_op jit(solution)/shard_map/ppermute | solution.py:15
  295.3 2.9 copy-start.2
  298.3 0.9 copy-start.6
  298.3 7.1 %copy-start.3 = (bf16[384,3,256]{0,2,1:T(8,128)(2,1)S(1)}, bf16[384,3,256]{0,2,1:T(8,128)(2,1)}, u32[]{:S(2)}) copy-start(bf16[384,3,256]{0,2,1:T(8,128)(2,1)} %copy.120) | copy-start | bytes 1769476
  299.9 19.3 %collective-permute-start.1 = (bf16[1,384,256]{2,1,0:T(8,128)(2,1)S(1)}, bf16[1,384,256]{2,1,0:T(8,128)(2,1)S(1)}, u32[]{:S(2)}, u32[]{:S(2)}) collective-permute-start(bf16[1,384,256]{2,1,0:T(8,128)(2,1)S(1)} %get-tuple-element.23), channel_id=1, source_target_pairs={{16,0},{32,16},{48,32},{64,48},{80,64},{96,80},{112,96},{128,112},... | collective-permute-start | bytes 589832 | tf_op jit(solution)/shard_map/ppermute | solution.py:15
Sparse Core Ops, SparseCore 0:
  19.4 62.5 all-gather.1
  156.6 138.6 all-reduce.2
